TPU v7x, 256 devices: a whole 4x4x8 slice. The times are simulated.
256 devices in a mesh: member: 8 (over y, z_hi), tile: 32 (over z_lo, x, core).
Axes of the slice: x: 4, y: 4, z: 8 (z_hi: 2, z_lo: 4; z = z_hi * 4 + z_lo), core: 2. Of those that a mesh axis runs over, the one named last changes fastest.
Arguments:
- surface: float32 [16, 1024, 512], P('member', 'tile'), may hold values from -6 to 6
- depth: float32 [1024, 512], P('tile'), may hold values from 0.32 to 0.45
- land: int32 [1024, 512], P('tile'), may hold values from 0 to 1, as said below
- gauge_cells: int32 [400], replicated, may hold values from 0 to 524287, as said below
- sigma: float32 [400], replicated, may hold values from 0.2 to 1
- observed: float32 [9600], replicated, may hold values from -4 to 4
- noise: float32 [16, 9600], P('member'), may hold values from -3 to 3
Outputs:
- updated: float32 [16, 1024, 512], P('member', 'tile')
- records: float32 [16, 9600], P('member', 'tile')
Inputs may be any that keep to these rules, and one draw needn't show every extreme that they name: `gauge_cells`: every block of 32 rows starting at a multiple of 32 holds a gauge in its first row and one in its last row. `land`: every gauge cell and the cells directly above and below it (rows taken periodically) are sea.
All inputs are finite; a program needn't handle non-finite values.
Results may differ from a plain program's by a relative error of at most 0.00022.
Values sent between devices are 32-bit elements; how exact they have to be, the bound alone decides.
A program may use at most 64 MiB of HBM per device.

v0:
```python
import jax
import jax.numpy as jnp
from jax import lax
from jax.sharding import PartitionSpec as P

STEPS = 24


def shifted(value, axis, steps):
    count = lax.axis_size(axis)
    pairs = [(source, (source + steps) % count) for source in range(count)]
    return lax.ppermute(value, axis, pairs)


def chol_solve(factor, rhs):
    middle = lax.linalg.triangular_solve(factor, rhs, left_side=True, lower=True, transpose_a=False)
    return lax.linalg.triangular_solve(factor, middle, left_side=True, lower=True, transpose_a=True)


def member_grams(gathered, weight):
    all_records, all_innovation = gathered
    anomaly = all_records - jnp.mean(all_records, axis=0, keepdims=True)
    weighted = anomaly * weight[None, :]
    gram_ss = jnp.dot(weighted, anomaly.T, precision=lax.Precision.HIGHEST)
    gram_se = jnp.dot(weighted, all_innovation.T, precision=lax.Precision.HIGHEST)
    return (gram_ss, gram_se)


def shards(surface, depth, land, gauge_cells, sigma, observed, noise):
    member_dev, row_count, col_count = surface.shape
    tile_count = lax.axis_size("tile")
    member_total = member_dev * lax.axis_size("member")
    wet_depth = depth * land.astype(jnp.float32)
    cell_count = row_count * col_count
    local_cell = gauge_cells - lax.axis_index("tile") * cell_count
    gauge_here = ((local_cell >= 0) & (local_cell < cell_count)).astype(jnp.float32)
    gauge_pos = jnp.clip(local_cell, 0, cell_count - 1)
    next_first = shifted(wet_depth[0:1], "tile", -1)
    zero_col = jnp.zeros((row_count, 1), jnp.float32)
    coeff_rows = jnp.minimum(wet_depth, jnp.concatenate([wet_depth[1:], next_first], 0))
    coeff_cols = jnp.minimum(wet_depth, jnp.concatenate([wet_depth[:, 1:], zero_col], 1))

    def advance(carry, ignored):
        level, flux_rows, flux_cols = carry
        next_row = shifted(level[:, 0:1, :], "tile", -1)
        member_rows = level.shape[0]
        below = jnp.concatenate([level[:, 1:], next_row], 1)
        flux_rows = flux_rows - coeff_rows * (below - level)
        level_col = jnp.zeros((member_rows, row_count, 1), jnp.float32)
        beside = jnp.concatenate([level[:, :, 1:], level_col], 2)
        flux_cols = flux_cols - coeff_cols * (beside - level)
        prior_row = shifted(flux_rows[:, -1:, :], "tile", 1)
        above = jnp.concatenate([prior_row, flux_rows[:, :-1]], 1)
        left = jnp.concatenate([level_col, flux_cols[:, :, :-1]], 2)
        level = level - (flux_rows - above + flux_cols - left)
        sample = jnp.take(level.reshape(member_dev, -1), gauge_pos, axis=1) * gauge_here[None, :]
        return ((level, flux_rows, flux_cols), sample)

    start = (surface, jnp.zeros_like(surface), jnp.zeros_like(surface))
    final, samples = lax.scan(advance, start, None, length=STEPS)
    partial_records = jnp.transpose(samples, (1, 0, 2)).reshape(member_dev, -1)
    data_count = partial_records.shape[1]
    piece_count = data_count // tile_count
    piece_start = lax.axis_index("tile") * piece_count
    weight = jnp.tile(1.0 / (sigma * sigma), data_count // sigma.shape[0])
    summed = lax.psum(partial_records, "tile")
    innovation = observed[None, :] + noise - summed
    gathered = (
        lax.all_gather(summed, "member", axis=0, tiled=True),
        lax.all_gather(innovation, "member", axis=0, tiled=True),
    )
    gram_ss, gram_se = member_grams(gathered, weight)
    out_records = lax.dynamic_slice_in_dim(summed, piece_start, piece_count, 1)
    identity = jnp.eye(member_total, dtype=jnp.float32)
    system = gram_ss + (member_total - 1.0) * identity
    factor = jnp.linalg.cholesky(system)
    mixing = chol_solve(factor, gram_se)
    combine = identity + mixing - jnp.mean(mixing, axis=0, keepdims=True)
    first_member = lax.axis_index("member") * member_dev
    local_combine = lax.dynamic_slice_in_dim(combine, first_member, member_dev, 1)
    updated = jnp.einsum(
        "kxy,km->mxy",
        lax.all_gather(surface, "member", axis=0, tiled=True),
        local_combine,
        precision=lax.Precision.HIGHEST,
    )
    return (updated, out_records)


def solution(mesh):
    in_specs = (
        P("member", "tile", None),
        P("tile", None),
        P("tile", None),
        P(),
        P(),
        P(),
        P("member", None),
    )
    out_specs = (P("member", "tile", None), P("member", "tile"))
    return jax.shard_map(shards, mesh=mesh, in_specs=in_specs, out_specs=out_specs, check_vma=False)
```

profile of v0, /device:TPU:128, one launch (start us, length us, event | category | flops | bytes accessed | tf_op | source)
XLA Modules:
  0.0 844.5 jit_solution(1827644809511835850)
XLA Ops:
  15.0 451.3 %while.17 = (s32[]{:T(128)}, f32[2,32,512]{2,1,0:T(8,128)S(1)}, f32[2,32,512]{2,1,0:T(8,128)S(1)}, f32[2,32,512]{2,1,0:T(8,128)S(1)}, f32[24,2,400]{1,2,0:T(8,12...) while((s32[]{:T(128)}, f32[2,32,512]{2,1,0:T(8,128)S(1)}, ...), condition=%wide.region_1.2_spmd.clone, body=%wide.region_0.1_spmd.clone.sunk | while | flops 464979 | bytes 2890483 | solution.py:60
  21.2 6.9 collective-permute-done.1
  28.2 4.6 copy.37
  39.8 6.9 collective-permute-done.1
  46.8 4.6 copy.37
  58.4 6.9 collective-permute-done.1
  65.4 4.6 copy.37
  77.0 6.9 collective-permute-done.1
  84.1 4.6 copy.37
  95.6 6.9 collective-permute-done.1
  102.7 4.6 copy.37
  114.2 6.9 collective-permute-done.1
  121.3 4.6 copy.37
  132.9 6.9 collective-permute-done.1
  139.9 4.6 copy.37
  151.5 6.9 collective-permute-done.1
  158.5 4.6 copy.37
  170.1 6.9 collective-permute-done.1
  177.1 4.6 copy.37
  188.7 6.9 collective-permute-done.1
  195.7 4.6 copy.37
  207.3 6.9 collective-permute-done.1
  214.3 4.6 copy.37
  225.9 6.9 collective-permute-done.1
  233.0 4.6 copy.37
  244.5 6.9 collective-permute-done.1
  251.6 4.6 copy.37
  263.1 6.9 collective-permute-done.1
  270.2 4.6 copy.37
  281.7 6.9 collective-permute-done.1
  288.8 4.6 copy.37
  300.3 6.9 collective-permute-done.1
  307.4 4.6 copy.37
  318.9 6.9 collective-permute-done.1
  326.0 4.6 copy.37
  337.6 6.9 collective-permute-done.1
  344.6 4.6 copy.37
  356.2 6.9 collective-permute-done.1
  363.2 4.6 copy.37
  374.8 6.9 collective-permute-done.1
  393.4 6.9 collective-permute-done.1
  400.4 4.6 copy.37
  412.0 6.9 collective-permute-done.1
  430.6 6.9 collective-permute-done.1
  449.2 6.9 collective-permute-done.1
  470.9 256.3 %all-reduce.5.cloned.1.call-done = f32[2,9600]{1,0:T(2,128)} async-done(((f32[2,9600]{1,0:T(2,128)}), f32[2,9600]{1,0:T(2,128)}) %all-reduce.5.cloned.1.call-update) | async-done | bytes 76816 | tf_op jit(solution)/shard_map/psum | solution.py:66
  727.2 48.0 %all-gather = f32[8,2,9600]{2,1,0:T(2,128)S(1)} all-gather(f32[1,2,9600]{2,1,0:T(2,128)} %bitcast.56), channel_id=1, replica_groups=mesh['member'=8,'tile'=32] {'member'}, dimensions={0}, use_global_device_ids=true | all-gather | bytes 691200 | tf_op jit(solution)/shard_map/all_gather | solution.py:69
  781.8 48.7 %all-gather.1 = f32[8,2,9600]{2,1,0:T(2,128)S(1)} all-gather(f32[1,2,9600]{2,1,0:T(2,128)S(1)} %subtract_bitcast_fusion), channel_id=1, replica_groups=mesh['member'=8,'tile'=32] {'member'}, dimensions={0}, use_global_device_ids=true | all-gather | bytes 691200 | tf_op jit(solution)/shard_map/all_gather | solution.py:70
  (392 shorter events, 215.7 us)
Async XLA Ops:
  8.0 719.2 %all-reduce.5.cloned.1.call-start = ((), (), s32[]{:S(2)}) async-start(), calls=%async_computation | async-start | bytes 153600 | tf_op jit(solution)/shard_map/psum | solution.py:66
  8.9 6.0 collective-permute-start.2
  15.0 5.9 collective-permute-start
  21.1 7.0 collective-permute-start.1
  38.2 1.3 collective-permute-start
  39.7 7.0 collective-permute-start.1
  56.8 1.3 collective-permute-start
  58.3 7.0 collective-permute-start.1
  75.5 1.3 collective-permute-start
  76.9 7.0 collective-permute-start.1
  94.1 1.3 collective-permute-start
  95.5 7.0 collective-permute-start.1
  114.1 7.0 collective-permute-start.1
  131.3 1.3 collective-permute-start
  132.8 7.0 collective-permute-start.1
  149.9 1.3 collective-permute-start
  151.4 7.0 collective-permute-start.1
  168.5 1.3 collective-permute-start
  170.0 7.0 collective-permute-start.1
  187.1 1.3 collective-permute-start
  188.6 7.0 collective-permute-start.1
  205.7 1.3 collective-permute-start
  207.2 7.0 collective-permute-start.1
  224.4 1.3 collective-permute-start
  225.8 7.0 collective-permute-start.1
  243.0 1.3 collective-permute-start
  244.4 7.0 collective-permute-start.1
  261.6 1.3 collective-permute-start
  263.0 7.0 collective-permute-start.1
  280.2 1.3 collective-permute-start
  281.6 7.0 collective-permute-start.1
  298.8 1.3 collective-permute-start
  300.2 7.0 collective-permute-start.1
  317.4 1.3 collective-permute-start
  318.8 7.0 collective-permute-start.1
  336.0 1.3 collective-permute-start
  337.5 7.0 collective-permute-start.1
  354.6 1.3 collective-permute-start
  356.1 7.0 collective-permute-start.1
  373.2 1.3 collective-permute-start
  374.7 7.0 collective-permute-start.1
  391.8 1.3 collective-permute-start
  393.3 7.0 collective-permute-start.1
  410.4 1.3 collective-permute-start
  411.9 7.0 collective-permute-start.1
  430.5 7.0 collective-permute-start.1
  449.1 7.0 collective-permute-start.1
  470.1 363.8 %all-gather.4.cloned.1.call-start = ((), (), s32[]{:S(2)}) async-start(), calls=%async_computation.1 | async-start | bytes 1179648 | tf_op jit(solution)/shard_map/all_gather | solution.py:83
  (6 other events, 632.5 us)
Sparse Core Ops, SparseCore 0:
  470.2 256.9 all-reduce.4
Sparse Core Ops, SparseCore 1:
  473.2 51.3 all-gather.3
where the time goes:
time: 846 us; the launch traced here: 844 us
  waiting for transfers between devices  451 us (53%)
  local copies, waits for them, and re-layouts  230 us (27%)
  blocking collectives  96.7 us (11%)
  other arithmetic  34.2 us (4%)
  between operations  15.6 us (2%)
  starting transfers between devices  10.4 us (1%)
    psum x1, waiting for transfers between devices, shards(): summed = lax.psum(partial_records, 'tile')  256 us
    ppermute x49, waiting for transfers between devices, shifted(): return lax.ppermute(value, axis, pairs)  194 us
    sub x24, local copies, waits for them, and re-layouts, advance(): level = level - (flux_rows - above + flux_cols - left)  111 us
    gather x24, local copies, waits for them, and re-layouts, advance(): jnp.take(level.reshape(member_dev, -1), gauge_pos, axis=1)  108 us
    all_gather x1, blocking collectives, shards(): lax.all_gather(innovation, 'member', axis=0, tiled=True)  48.7 us
    all_gather x1, blocking collectives, shards(): lax.all_gather(summed, 'member', axis=0, tiled=True)  48 us
    dynamic_update_slice x24, other arithmetic, shards(): final, samples = lax.scan(advance, start, None, length=STEPS)  20.8 us
  transfers between devices with their start and end apart: 51, of which 49 were waited for; matrix products, arithmetic and copies ran while one was open for 2% of the time, Pallas kernels for 0%

commit v1 on v0

--- a/solution.py
+++ b/solution.py
@@ -4,6 +4,11 @@
 from jax.sharding import PartitionSpec as P
 
 STEPS = 24
+
+
+def gather_over(shard, mesh_axis, d):
+    sent = jnp.stack([shard] * lax.axis_size(mesh_axis))
+    return jnp.concatenate(lax.all_to_all(sent, mesh_axis, 0, 0), axis=d)
 
 
 def shifted(value, axis, steps):
@@ -67,7 +72,7 @@
     innovation = observed[None, :] + noise - summed
     gathered = (
         lax.all_gather(summed, "member", axis=0, tiled=True),
-        lax.all_gather(innovation, "member", axis=0, tiled=True),
+        gather_over(innovation, "member", 0),
     )
     gram_ss, gram_se = member_grams(gathered, weight)
     out_records = lax.dynamic_slice_in_dim(summed, piece_start, piece_count, 1)

time: 846 us -> 819 us (0.968)
  blocking collectives: 96.7 us -> 53.7 us
  starting transfers between devices: 10.4 us -> 19.9 us
    all_gather x1 -> x0, blocking collectives: 48.7 us -> none  [shards(): lax.all_gather(innovation, 'member', axis=0, tiled=True)]
    all_to_all x0 -> x1, starting transfers between devices: none -> 9.51 us  [gather_over(): return jnp.concatenate(lax.all_to_all(sent, mesh_axis, 0, 0), axis=d)]
  transfers between devices with their start and end apart: 51 -> 52, of which waited for: 49 -> 50; matrix products, arithmetic and copies ran while one was open for 2% -> 2% of each run, Pallas kernels for 0% -> 0%
where the time goes in v1:
time: 819 us; the launch traced here: 813 us
  waiting for transfers between devices  452 us (55%)
  local copies, waits for them, and re-layouts  231 us (28%)
  blocking collectives  53.7 us (7%)
  other arithmetic  34.2 us (4%)
  starting transfers between devices  19.9 us (2%)
  between operations  15.6 us (2%)
    psum x1, waiting for transfers between devices, shards(): summed = lax.psum(partial_records, 'tile')  256 us
    ppermute x49, waiting for transfers between devices, shifted(): return lax.ppermute(value, axis, pairs)  194 us
    sub x24, local copies, waits for them, and re-layouts, advance(): level = level - (flux_rows - above + flux_cols - left)  111 us
    gather x24, local copies, waits for them, and re-layouts, advance(): jnp.take(level.reshape(member_dev, -1), gauge_pos, axis=1)  108 us
    all_gather x1, blocking collectives, shards(): lax.all_gather(summed, 'member', axis=0, tiled=True)  53.7 us
    dynamic_update_slice x24, other arithmetic, shards(): final, samples = lax.scan(advance, start, None, length=STEPS)  20.8 us
  transfers between devices with their start and end apart: 52, of which 50 were waited for; matrix products, arithmetic and copies ran while one was open for 2% of the time, Pallas kernels for 0%

profile of v1, /device:TPU:128, one launch (start us, length us, event | category | flops | bytes accessed | tf_op | source)
XLA Modules:
  0.0 812.8 jit_solution(15311462430397097585)
XLA Ops:
  15.0 451.2 %while.17 = (s32[]{:T(128)}, f32[2,32,512]{2,1,0:T(8,128)S(1)}, f32[2,32,512]{2,1,0:T(8,128)S(1)}, f32[2,32,512]{2,1,0:T(8,128)S(1)}, f32[24,2,400]{1,2,0:T(8,12...) while((s32[]{:T(128)}, f32[2,32,512]{2,1,0:T(8,128)S(1)}, ...), condition=%wide.region_1.2_spmd.clone, body=%wide.region_0.1_spmd.clone.sunk | while | flops 464979 | bytes 2890483 | solution.py:65
  21.2 6.9 collective-permute-done.1
  28.2 4.6 copy.37
  39.8 6.9 collective-permute-done.1
  46.8 4.6 copy.37
  58.4 6.9 collective-permute-done.1
  65.4 4.6 copy.37
  77.0 6.9 collective-permute-done.1
  84.1 4.6 copy.37
  95.6 6.9 collective-permute-done.1
  102.7 4.6 copy.37
  114.3 6.9 collective-permute-done.1
  121.3 4.6 copy.37
  132.9 6.9 collective-permute-done.1
  139.9 4.6 copy.37
  151.5 6.9 collective-permute-done.1
  158.5 4.6 copy.37
  170.1 6.9 collective-permute-done.1
  177.1 4.6 copy.37
  188.7 6.9 collective-permute-done.1
  195.7 4.6 copy.37
  207.3 6.9 collective-permute-done.1
  214.3 4.6 copy.37
  225.9 6.9 collective-permute-done.1
  232.9 4.6 copy.37
  244.5 6.9 collective-permute-done.1
  251.5 4.6 copy.37
  263.1 6.9 collective-permute-done.1
  270.1 4.6 copy.37
  281.7 6.9 collective-permute-done.1
  288.7 4.6 copy.37
  300.3 6.9 collective-permute-done.1
  307.3 4.6 copy.37
  318.9 6.9 collective-permute-done.1
  325.9 4.6 copy.37
  337.5 6.9 collective-permute-done.1
  344.5 4.6 copy.37
  356.1 6.9 collective-permute-done.1
  363.1 4.6 copy.37
  374.7 6.9 collective-permute-done.1
  381.7 4.6 copy.37
  393.3 6.9 collective-permute-done.1
  411.9 6.9 collective-permute-done.1
  430.5 6.9 collective-permute-done.1
  449.1 6.9 collective-permute-done.1
  470.8 256.3 %all-reduce.5.cloned.1.call-done = f32[2,9600]{1,0:T(2,128)} async-done(((f32[2,9600]{1,0:T(2,128)}), f32[2,9600]{1,0:T(2,128)}) %all-reduce.5.cloned.1.call-update) | async-done | bytes 76816 | tf_op jit(solution)/shard_map/psum | solution.py:71
  727.1 53.7 %all-gather = f32[8,2,9600]{2,1,0:T(2,128)S(1)} all-gather(f32[1,2,9600]{2,1,0:T(2,128)} %bitcast.54), channel_id=1, replica_groups=mesh['member'=8,'tile'=32] {'member'}, dimensions={0}, use_global_device_ids=true | all-gather | bytes 691200 | tf_op jit(solution)/shard_map/all_gather | solution.py:74
  782.7 9.5 %all-to-all-start = ((f32[8,2,9600]{2,1,0:T(2,128)}), f32[8,2,9600]{2,1,0:T(2,128)S(1)}, u32[]{:S(2)}, u32[]{:S(2)}) async-start(f32[8,2,9600]{2,1,0:T(2,128)} %stack.2), calls=%async_computation | async-start | bytes 1228800 | tf_op jit(solution)/shard_map/all_to_all | solution.py:11
  (394 shorter events, 217.7 us)
Async XLA Ops:
  8.0 719.1 %all-reduce.5.cloned.1.call-start = ((), (), s32[]{:S(2)}) async-start(), calls=%async_computation.1 | async-start | bytes 153600 | tf_op jit(solution)/shard_map/psum | solution.py:71
  8.9 6.0 collective-permute-start.2
  15.0 5.9 collective-permute-start
  21.1 7.0 collective-permute-start.1
  38.2 1.3 collective-permute-start
  39.7 7.0 collective-permute-start.1
  56.8 1.3 collective-permute-start
  58.3 7.0 collective-permute-start.1
  75.5 1.3 collective-permute-start
  76.9 7.0 collective-permute-start.1
  94.1 1.3 collective-permute-start
  95.5 7.0 collective-permute-start.1
  112.7 1.3 collective-permute-start
  114.1 7.0 collective-permute-start.1
  131.3 1.3 collective-permute-start
  132.7 7.0 collective-permute-start.1
  149.9 1.3 collective-permute-start
  151.4 7.0 collective-permute-start.1
  168.5 1.3 collective-permute-start
  170.0 7.0 collective-permute-start.1
  187.1 1.3 collective-permute-start
  188.5 7.0 collective-permute-start.1
  205.7 1.3 collective-permute-start
  207.2 7.0 collective-permute-start.1
  224.3 1.3 collective-permute-start
  225.8 7.0 collective-permute-start.1
  242.9 1.3 collective-permute-start
  244.4 7.0 collective-permute-start.1
  261.5 1.3 collective-permute-start
  263.0 7.0 collective-permute-start.1
  280.1 1.3 collective-permute-start
  281.6 7.0 collective-permute-start.1
  298.7 1.3 collective-permute-start
  300.2 7.0 collective-permute-start.1
  317.3 1.3 collective-permute-start
  318.8 7.0 collective-permute-start.1
  335.9 1.3 collective-permute-start
  337.4 7.0 collective-permute-start.1
  354.5 1.3 collective-permute-start
  356.0 7.0 collective-permute-start.1
  373.1 1.3 collective-permute-start
  374.6 7.0 collective-permute-start.1
  393.2 7.0 collective-permute-start.1
  411.8 7.0 collective-permute-start.1
  430.4 7.0 collective-permute-start.1
  449.0 7.0 collective-permute-start.1
  470.0 332.2 %all-gather.3.cloned.1.call-start = ((), (), s32[]{:S(2)}) async-start(), calls=%async_computation.2 | async-start | bytes 1179648 | tf_op jit(solution)/shard_map/all_gather | solution.py:88
  782.7 17.5 %all-to-all-start = ((f32[8,2,9600]{2,1,0:T(2,128)}), f32[8,2,9600]{2,1,0:T(2,128)S(1)}, u32[]{:S(2)}, u32[]{:S(2)}) async-start(f32[8,2,9600]{2,1,0:T(2,128)} %stack.2), calls=%async_computation | async-start | bytes 1228800 | tf_op jit(solution)/shard_map/all_to_all | solution.py:11
  (7 other events, 638.9 us)
Sparse Core Ops, SparseCore 0:
  470.2 256.9 all-reduce.4
Sparse Core Ops, SparseCore 1:
  473.1 51.3 all-gather.2
